TPU v7x, 32 devices: a whole 2x2x4 slice. The times are simulated.
32 devices in a mesh: strip: 8 (over y, x, core), mode: 4 (over z).
Axes of the slice: x: 2, y: 2, z: 4, core: 2. Of those that a mesh axis runs over, the one named last changes fastest.
Arguments:
- object_field: float32 [2, 2048, 384], P(None, 'strip'), may hold values from -5 to 5
- probe_modes: float32 [2, 8, 256, 256], P(None, 'mode'), may hold values from -2.5 to 2.5
- measured: float32 [8, 4, 256, 256], P('strip'), may hold values from 0.1 to 27
- positions: int32 [8, 4, 2], P('strip'), may hold values from 0 to 128, as said below
Outputs:
- object_new: float32 [2, 2048, 384], P(None, 'strip')
Inputs may be any that keep to these rules, and one draw needn't show every extreme that they name: positions[s,k,0] is the first row of window k within strip s and positions[s,k,1] its first column; the windows of every strip form a two by two raster with small offsets: windows 0 and 3 start at row 128, windows 1 and 2 at row 0, window 1 at column 128, window 3 at most 16 columns left of it, windows 0 and 2 at columns 0 to 16.
All inputs are finite; a program needn't handle non-finite values.
Results may differ from a plain program's by a relative error of at most 0.0001.
Values sent between devices are 32-bit elements; how exact they have to be, the bound alone decides.
A program may use at most 128 MiB of HBM per device.

v0:
```python
import jax
import jax.numpy as jnp
from jax import lax
from jax.sharding import PartitionSpec as P

HALO = 128
ITERS = 3


regularizer = 0.1
step_scale = 0.3
epsilon = 1e-06
highest = lax.Precision.HIGHEST


def from_behind(block, axis, distance):
    devices = range(lax.axis_size(axis))
    route = [(i - distance, i) for i in devices if i - distance in devices]
    return lax.ppermute(block, axis, route)


def dft_tables(length):
    indices = jnp.arange(length, dtype=jnp.int32)
    phases = indices[:, None] * indices[None, :] % length
    angles = phases.astype(jnp.float32) * (2.0 * jnp.pi / length)
    scaling = 1.0 / jnp.sqrt(jnp.float32(length))
    return (jnp.cos(angles) * scaling, -jnp.sin(angles) * scaling)


def transform(part_real, part_imag, cosine_table, sine_table):
    length = cosine_table.shape[0]
    stacked_rows = jnp.concatenate([cosine_table, sine_table], axis=0)
    left_real = jnp.einsum("jk,bkl->bjl", stacked_rows, part_real, precision=highest)
    left_imag = jnp.einsum("jk,bkl->bjl", stacked_rows, part_imag, precision=highest)
    middle_real = left_real[:, :length] - left_imag[:, length:]
    middle_imag = left_imag[:, :length] + left_real[:, length:]
    stacked_cols = jnp.concatenate([cosine_table, sine_table], axis=1)
    right_real = jnp.einsum("bjk,kl->bjl", middle_real, stacked_cols, precision=highest)
    right_imag = jnp.einsum("bjk,kl->bjl", middle_imag, stacked_cols, precision=highest)
    return (
        right_real[..., :length] - right_imag[..., length:],
        right_imag[..., :length] + right_real[..., length:],
    )


def body(object_field, probe_modes, measured, positions):
    stripe_rows = object_field.shape[1]
    width_cols = object_field.shape[2]
    window = probe_modes.shape[2]
    local_modes = probe_modes.shape[1]
    slots = positions.shape[1]
    halo_rows = HALO
    cosine_table, sine_table = dft_tables(window)
    rows_at = positions[0, :, 0]
    cols_at = positions[0, :, 1]
    total_cells = stripe_rows * lax.axis_size("strip") * width_cols
    measured_intensity = measured[0]
    probe_real = probe_modes[0][None]
    probe_imag = probe_modes[1][None]
    zero_index = jnp.zeros((), jnp.int32)
    for iteration in range(ITERS):
        below = from_behind(object_field[:, :halo_rows], "strip", -1)
        frame = jnp.concatenate([object_field, below], axis=1)
        patches = jnp.stack(
            [
                lax.dynamic_slice(
                    frame, (zero_index, rows_at[slot], cols_at[slot]), (2, window, window)
                )
                for slot in range(slots)
            ],
            axis=1,
        )
        patch_real = patches[0][:, None]
        patch_imag = patches[1][:, None]
        exit_real = probe_real * patch_real - probe_imag * patch_imag
        exit_imag = probe_real * patch_imag + probe_imag * patch_real
        far_real, far_imag = transform(
            exit_real.reshape(-1, window, window),
            exit_imag.reshape(-1, window, window),
            cosine_table,
            sine_table,
        )
        far_real = far_real.reshape(slots, local_modes, window, window)
        far_imag = far_imag.reshape(slots, local_modes, window, window)
        probe_power = jnp.sum(far_real * far_real + far_imag * far_imag, axis=1)
        summed_power = lax.psum(probe_power, "mode")
        object_update = (
            jnp.sqrt((measured_intensity + regularizer) / (summed_power + regularizer)) - 1.0
        )
        shift_real = (object_update[:, None] * far_real).reshape(-1, window, window)
        shift_imag = (object_update[:, None] * far_imag).reshape(-1, window, window)
        delta_real, delta_imag = transform(shift_real, shift_imag, cosine_table, -sine_table)
        delta_real = delta_real.reshape(slots, local_modes, window, window)
        delta_imag = delta_imag.reshape(slots, local_modes, window, window)
        grad_real = jnp.sum(probe_real * delta_real + probe_imag * delta_imag, axis=1)
        grad_imag = jnp.sum(probe_real * delta_imag - probe_imag * delta_real, axis=1)
        grad_real, grad_imag = lax.psum((grad_real, grad_imag), "mode")
        frame_grad = jnp.zeros((2, stripe_rows + halo_rows, width_cols), jnp.float32)
        for slot in range(slots):
            start = (zero_index, rows_at[slot], cols_at[slot])
            current = lax.dynamic_slice(frame_grad, start, (2, window, window))
            frame_grad = lax.dynamic_update_slice(
                frame_grad, current + jnp.stack([grad_real[slot], grad_imag[slot]]), start
            )
        arrived = from_behind(frame_grad[:, stripe_rows:], "strip", 1)
        gradient = jnp.concatenate(
            [frame_grad[:, :halo_rows] + arrived, frame_grad[:, halo_rows:stripe_rows]], axis=1
        )
        square_sum = lax.psum(jnp.sum(gradient * gradient), "strip")
        step_factor = step_scale / jnp.sqrt(square_sum / total_cells + epsilon)
        object_field = object_field + step_factor * gradient
    return object_field


def solution(mesh):
    return jax.shard_map(
        body,
        mesh=mesh,
        in_specs=(
            P(None, "strip", None),
            P(None, "mode", None, None),
            P("strip", None, None, None),
            P("strip", None, None),
        ),
        out_specs=P(None, "strip", None),
        check_vma=False,
    )
```

profile of v0, /device:TPU:0, one launch (start us, length us, event | category | flops | bytes accessed | tf_op | source)
XLA Modules:
  0.0 812.3 jit_solution(13496103538297187486)
XLA Ops:
  6.5 1.9 slice.359
  9.7 1.6 fusion.111
  30.1 7.1 convolution_bitcast_fusion.10
  37.2 7.5 convolution_bitcast_fusion.11
  44.8 3.7 fusion.22
  48.5 3.7 fusion.20
  52.2 1.9 copy-done.1
  54.2 1.8 bitcast_reduce_fusion.2
  57.0 54.5 %all-reduce.10.cloned.1.call-done = f32[4,256,256]{2,1,0:T(8,128)} async-done(((f32[4,256,256]{2,1,0:T(8,128)}), f32[4,256,256]{2,1,0:T(8,128)}) %all-reduce.10.cloned.1.call-update) | async-done | bytes 1048592 | tf_op jit(solution)/shard_map/psum | solution.py:86
  113.2 4.1 bitcast_multiply_fusion.5
  117.2 7.2 convolution_bitcast_fusion.9
  124.5 7.6 convolution_bitcast_fusion.8
  132.1 3.7 fusion.16
  135.8 3.7 fusion.18
  139.4 2.1 add_reduce_fusion.2
  141.6 85.5 %all-reduce.20.cloned.1.call-done = (f32[4,256,256]{2,1,0:T(8,128)}, f32[4,256,256]{2,1,0:T(8,128)}) async-done(((f32[4,256,256]{2,1,0:T(8,128)}, f32[4,256,256]{2,1,0:T(8,128)}), (f32[4,256,256]{2,1,0:T(8,128)}, f32[4,256,256]{2,1,0:T(8,128)})) %all-reduce.20.cloned.1.call-update) | async-done | bytes 2097168 | tf_op jit(solution)/shard_map/psum | solution.py:97
  227.1 2.2 fusion.109
  230.3 6.6 dynamic_update_slice.36
  238.2 5.3 dynamic_update_slice.37
  244.7 8.1 dynamic_update_slice.38
  254.0 6.6 dynamic_update_slice.39
  265.0 18.3 %psum.87 = f32[]{:T(128)} all-reduce(f32[]{:T(128)} %multiply_reduce_fusion.2), channel_id=1, replica_groups=mesh['strip'=8,'mode'=4] {'strip'}, use_global_device_ids=true, to_apply=%region_7.8 | all-reduce | flops 1 | bytes 8 | tf_op jit(solution)/shard_map/psum | solution.py:109
  286.8 2.1 collective-permute-done.2
  291.0 7.1 convolution_bitcast_fusion.6
  298.1 7.3 convolution_bitcast_fusion.7
  305.4 3.7 fusion.14
  309.1 3.7 fusion.12
  312.9 1.9 copy-done.5
  316.9 56.2 %all-reduce.12.cloned.1.call-done = f32[4,256,256]{2,1,0:T(8,128)} async-done(((f32[4,256,256]{2,1,0:T(8,128)}), f32[4,256,256]{2,1,0:T(8,128)}) %all-reduce.12.cloned.1.call-update) | async-done | bytes 1048592 | tf_op jit(solution)/shard_map/psum | solution.py:86
  374.8 4.1 bitcast_multiply_fusion.3
  378.9 7.2 convolution_bitcast_fusion.5
  386.1 7.4 convolution_bitcast_fusion.4
  393.5 3.7 fusion.8
  397.1 3.7 fusion.10
  400.8 2.1 add_reduce_fusion.1
  403.0 85.5 %all-reduce.18.cloned.1.call-done = (f32[4,256,256]{2,1,0:T(8,128)}, f32[4,256,256]{2,1,0:T(8,128)}) async-done(((f32[4,256,256]{2,1,0:T(8,128)}, f32[4,256,256]{2,1,0:T(8,128)}), (f32[4,256,256]{2,1,0:T(8,128)}, f32[4,256,256]{2,1,0:T(8,128)})) %all-reduce.18.cloned.1.call-update) | async-done | bytes 2097168 | tf_op jit(solution)/shard_map/psum | solution.py:97
  488.5 2.2 fusion.107
  491.7 6.6 dynamic_update_slice.40
  499.6 5.3 dynamic_update_slice.41
  506.1 8.1 dynamic_update_slice.42
  515.4 6.6 dynamic_update_slice.43
  526.4 18.3 %psum.91 = f32[]{:T(128)} all-reduce(f32[]{:T(128)} %multiply_reduce_fusion.1), channel_id=1, replica_groups=mesh['strip'=8,'mode'=4] {'strip'}, use_global_device_ids=true, to_apply=%region_15.16 | all-reduce | flops 1 | bytes 8 | tf_op jit(solution)/shard_map/psum | solution.py:109
  546.7 1.7 collective-permute-start.4
  548.4 1.9 collective-permute-done.4
  552.4 7.1 convolution_bitcast_fusion.2
  559.5 7.2 convolution_bitcast_fusion.3
  566.8 3.7 fusion.6
  570.5 3.7 fusion.4
  574.2 1.9 copy-done.3
  578.0 56.5 %all-reduce.14.cloned.1.call-done = f32[4,256,256]{2,1,0:T(8,128)} async-done(((f32[4,256,256]{2,1,0:T(8,128)}), f32[4,256,256]{2,1,0:T(8,128)}) %all-reduce.14.cloned.1.call-update) | async-done | bytes 1048592 | tf_op jit(solution)/shard_map/psum | solution.py:86
  634.5 2.0 fusion.29
  636.5 4.1 bitcast_multiply_fusion.1
  640.5 7.2 convolution_bitcast_fusion.1
  647.8 7.6 convolution_bitcast_fusion
  655.4 3.7 fusion
  659.0 3.7 fusion.2
  662.7 2.1 add_reduce_fusion
  664.8 85.6 %all-reduce.16.cloned.1.call-done = (f32[4,256,256]{2,1,0:T(8,128)}, f32[4,256,256]{2,1,0:T(8,128)}) async-done(((f32[4,256,256]{2,1,0:T(8,128)}, f32[4,256,256]{2,1,0:T(8,128)}), (f32[4,256,256]{2,1,0:T(8,128)}, f32[4,256,256]{2,1,0:T(8,128)})) %all-reduce.16.cloned.1.call-update) | async-done | bytes 2097168 | tf_op jit(solution)/shard_map/psum | solution.py:97
  750.4 2.1 fusion.105
  753.4 6.8 dynamic_update_slice.44
  761.4 5.3 dynamic_update_slice.45
  766.9 8.1 dynamic_update_slice.46
  775.2 6.6 dynamic_update_slice.47
  785.3 18.2 %psum.95 = f32[]{:T(128)} all-reduce(f32[]{:T(128)} %multiply_reduce_fusion), channel_id=1, replica_groups=mesh['strip'=8,'mode'=4] {'strip'}, use_global_device_ids=true, to_apply=%region_23.24 | all-reduce | flops 1 | bytes 8 | tf_op jit(solution)/shard_map/psum | solution.py:109
  (101 shorter events, 46.9 us)
Async XLA Ops:
  6.5 21.9 %copy-start.11 = (f32[2,2,256,256]{3,2,1,0:T(8,128)S(1)}, f32[2,2,256,256]{3,2,1,0:T(8,128)}, u32[]{:S(2)}) copy-start(f32[2,2,256,256]{3,2,1,0:T(8,128)} %param.5) | copy-start | bytes 3145732
  6.5 105.0 %all-reduce.10.cloned.1.call-start = ((), (), s32[]{:S(2)}) async-start(), calls=%async_computation | async-start | bytes 2097152 | tf_op jit(solution)/shard_map/psum | solution.py:86
  8.4 20.2 %collective-permute-start = (f32[2,128,384]{2,1,0:T(8,128)}, f32[2,128,384]{2,1,0:T(8,128)S(1)}, u32[]{:S(2)}, u32[]{:S(2)}) collective-permute-start(f32[2,128,384]{2,1,0:T(8,128)} %slice.359), channel_id=1, source_target_pairs={{4,0},{8,4},{12,8},{16,12},{20,16},{24,20},{28,24},{5,1},{9,5},{13... | collective-permute-start | bytes 1179656 | tf_op jit(solution)/shard_map/ppermute | solution.py:19
  48.5 3.7 copy-start
  52.2 1.9 copy-start.1
  54.2 57.3 %copy-start.7 = (f32[1,4,256,256]{3,2,1,0:T(8,128)S(1)}, f32[1,4,256,256]{3,2,1,0:T(8,128)}, u32[]{:S(2)}) copy-start(f32[1,4,256,256]{3,2,1,0:T(8,128)} %param.6) | copy-start | bytes 3145732
  56.0 171.2 %all-reduce.20.cloned.1.call-start = ((), (), s32[]{:S(2)}) async-start(), calls=%async_computation.5 | async-start | bytes 4194304 | tf_op jit(solution)/shard_map/psum | solution.py:97
  141.5 231.6 %all-reduce.12.cloned.1.call-start = ((), (), s32[]{:S(2)}) async-start(), calls=%async_computation.1 | async-start | bytes 2097152 | tf_op jit(solution)/shard_map/psum | solution.py:86
  227.1 2.2 copy-start.12
  260.7 2.6 collective-permute-start.1
  263.4 0.7 copy-start.10
  285.2 5.0 copy-start.6
  285.3 3.6 collective-permute-start.2
  309.1 3.7 copy-start.4
  312.8 1.9 copy-start.5
  314.8 58.4 %copy-start.8 = (f32[1,4,256,256]{3,2,1,0:T(8,128)S(1)}, f32[1,4,256,256]{3,2,1,0:T(8,128)}, u32[]{:S(2)}) copy-start(f32[1,4,256,256]{3,2,1,0:T(8,128)} %param.6) | copy-start | bytes 3145732
  316.4 172.1 %all-reduce.18.cloned.1.call-start = ((), (), s32[]{:S(2)}) async-start(), calls=%async_computation.4 | async-start | bytes 4194304 | tf_op jit(solution)/shard_map/psum | solution.py:97
  402.9 231.6 %all-reduce.14.cloned.1.call-start = ((), (), s32[]{:S(2)}) async-start(), calls=%async_computation.2 | async-start | bytes 2097152 | tf_op jit(solution)/shard_map/psum | solution.py:86
  488.5 2.2 copy-start.13
  522.1 2.6 collective-permute-start.3
  524.8 0.7 copy-start.9
  546.7 3.6 collective-permute-start.4
  570.5 3.7 copy-start.2
  574.2 1.9 copy-start.3
  577.8 172.7 %all-reduce.16.cloned.1.call-start = ((), (), s32[]{:S(2)}) async-start(), calls=%async_computation.3 | async-start | bytes 4194304 | tf_op jit(solution)/shard_map/psum | solution.py:97
  750.4 2.1 copy-start.14
  781.8 2.6 collective-permute-start.5
Sparse Core Ops, SparseCore 0:
  56.1 55.3 all-reduce.9
  141.7 85.4 all-reduce.19
  316.5 56.5 all-reduce.11
  403.0 85.4 all-reduce.17
  577.9 56.5 all-reduce.13
  664.9 85.4 all-reduce.15
where the time goes:
time: 822 us; the launch traced here: 812 us
  waiting for transfers between devices  432 us (53%)
  matrix products  132 us (16%)
  local copies, waits for them, and re-layouts  102 us (12%)
  blocking collectives  54.9 us (7%)
  other arithmetic  50.7 us (6%)
  between operations  31.3 us (4%)
  starting transfers between devices  9.27 us (1%)
    psum x3, waiting for transfers between devices, body(): grad_real, grad_imag = lax.psum((grad_real, grad_imag), 'mode')  257 us
    psum x3, waiting for transfers between devices, body(): summed_power = lax.psum(probe_power, 'mode')  167 us
    dynamic_update_slice x12, local copies, waits for them, and re-layouts, body(): lax.dynamic_update_slice(frame_grad, current + jnp.stack([grad_real[slot]...  79.7 us
    psum x3, blocking collectives, body(): square_sum = lax.psum(jnp.sum(gradient * gradient), 'strip')  54.9 us
    dot_general x6, matrix products, transform(): jnp.einsum('jk,bkl->bjl', stacked_rows, part_imag, precision=highest)  43.8 us
    dot_general x6, matrix products, transform(): jnp.einsum('jk,bkl->bjl', stacked_rows, part_real, precision=highest)  43.7 us
    dot_general x6, matrix products, transform(): jnp.einsum('bjk,kl->bjl', middle_real, stacked_cols, precision=highest)  22.2 us
    dot_general x6, matrix products, transform(): jnp.einsum('bjk,kl->bjl', middle_imag, stacked_cols, precision=highest)  22.2 us
  transfers between devices with their start and end apart: 12, of which 11 were waited for; matrix products, arithmetic and copies ran while one was open for 1% of the time, Pallas kernels for 0%

commit v1 on v0

v1 whole, which is shorter than its diff:
```python
import functools

import jax
import jax.numpy as jnp
import numpy as np
from jax import lax
from jax.experimental import pallas as pl
from jax.experimental.pallas import tpu as pltpu
from jax.sharding import PartitionSpec as P

HALO = 128
ITERS = 3

regularizer = 0.1
step_scale = 0.3
epsilon = 1e-06
f32 = jnp.float32
bf16 = jnp.bfloat16


def tables(n):
    half = n // 2
    k = np.arange(half)
    angle = 2.0 * np.pi * (np.outer(k, k) % half) / half
    c = np.cos(angle) / np.sqrt(n)
    s = np.sin(angle) / np.sqrt(n)
    right_f = np.block([[c, -s], [s, c]])
    right_i = np.block([[c, s], [-s, c]])
    turn = 2.0 * np.pi * k / n
    wr, wi = np.cos(turn), -np.sin(turn)

    def split(t):
        t = jnp.asarray(t, f32)
        high = t.astype(bf16)
        low = (t - high.astype(f32)).astype(bf16)
        return high, low

    rf, ri = split(right_f), split(right_i)
    lf, li = split(right_f.T), split(right_i.T)
    rights = jnp.stack([rf[0], rf[1], ri[0], ri[1]])
    lefts = jnp.stack([jnp.concatenate(lf), jnp.concatenate(li)])
    lanes = jnp.asarray(np.stack([wr, wi]), f32)[:, None, :]
    subs = jnp.asarray(np.broadcast_to(np.stack([wr, wi])[:, :, None], (2, half, n)), f32)
    return rights, lefts, lanes, subs


def split2(x):
    high = x.astype(bf16)
    low = (x - high.astype(f32)).astype(bf16)
    return high, low


def dot(a, b):
    return jnp.dot(a, b, preferred_element_type=f32)


def right_dot(x, t_high, t_low):
    high, low = split2(x)
    return dot(high, t_high) + (dot(low, t_high) + dot(high, t_low))


def left_dot(t_both, x):
    n = x.shape[0]
    high, low = split2(x)
    both = dot(t_both, high)
    return both[:n] + (both[n:] + dot(t_both[:n], low))


def gradient_kernel(col_ref, obj_ref, probe_ref, meas_ref, rights, lefts, lanes, subs, out_ref, far_ref, power_ref, acc_ref, patch_ref):
    n = meas_ref.shape[0]
    half = n // 2
    width = obj_ref.shape[2]
    modes = probe_ref.shape[1]
    col = col_ref[0]
    back = jnp.where(col == 0, 0, width - col)
    for part in range(2):
        patch_ref[part] = pltpu.roll(obj_ref[part], back, 1)[:, :n]
    power_ref[...] = jnp.zeros_like(power_ref)
    acc_ref[...] = jnp.zeros_like(acc_ref)
    cat = jnp.concatenate

    def forward(m):
        pr, pi = probe_ref[0, m], probe_ref[1, m]
        xr, xi = patch_ref[0], patch_ref[1]
        er = pr * xr - pi * xi
        ei = pr * xi + pi * xr
        wr, wi = lanes[0], lanes[1]
        ar, ai = er[:, :half] + er[:, half:], ei[:, :half] + ei[:, half:]
        br, bi = er[:, :half] - er[:, half:], ei[:, :half] - ei[:, half:]
        even = right_dot(cat([ar, ai], 1), rights[0], rights[1])
        odd = right_dot(cat([br * wr - bi * wi, br * wi + bi * wr], 1), rights[0], rights[1])
        yr = cat([even[:, :half], odd[:, :half]], 1)
        yi = cat([even[:, half:], odd[:, half:]], 1)
        wr, wi = subs[0], subs[1]
        ar, ai = yr[:half] + yr[half:], yi[:half] + yi[half:]
        br, bi = yr[:half] - yr[half:], yi[:half] - yi[half:]
        even = left_dot(lefts[0], cat([ar, ai], 0))
        odd = left_dot(lefts[0], cat([br * wr - bi * wi, br * wi + bi * wr], 0))
        far_ref[m, 0] = even
        far_ref[m, 1] = odd
        return cat(
            [
                even[:half] * even[:half] + even[half:] * even[half:],
                odd[:half] * odd[:half] + odd[half:] * odd[half:],
            ],
            0,
        )

    def forward_two(i, carry):
        power_ref[...] += forward(2 * i) + forward(2 * i + 1)
        return carry

    lax.fori_loop(0, modes // 2, forward_two, 0)
    power_ref[...] = jnp.sqrt((meas_ref[...] + regularizer) / (power_ref[...] + regularizer)) - 1.0

    def backward(m):
        ce, co = power_ref[:half], power_ref[half:]
        ce, co = cat([ce, ce], 0), cat([co, co], 0)
        even = left_dot(lefts[1], ce * far_ref[m, 0])
        odd = left_dot(lefts[1], co * far_ref[m, 1])
        wr, wi = subs[0], subs[1]
        ar, ai = even[:half], even[half:]
        br, bi = odd[:half], odd[half:]
        tr, ti = br * wr + bi * wi, bi * wr - br * wi
        yr = cat([ar + tr, ar - tr], 0)
        yi = cat([ai + ti, ai - ti], 0)
        even = right_dot(cat([yr[:, :half], yi[:, :half]], 1), rights[2], rights[3])
        odd = right_dot(cat([yr[:, half:], yi[:, half:]], 1), rights[2], rights[3])
        wr, wi = lanes[0], lanes[1]
        ar, ai = even[:, :half], even[:, half:]
        br, bi = odd[:, :half], odd[:, half:]
        tr, ti = br * wr + bi * wi, bi * wr - br * wi
        dr = cat([ar + tr, ar - tr], 1)
        di = cat([ai + ti, ai - ti], 1)
        pr, pi = probe_ref[0, m], probe_ref[1, m]
        return pr * dr + pi * di, pr * di - pi * dr

    def backward_two(i, carry):
        gr, gi = backward(2 * i)
        hr, hi = backward(2 * i + 1)
        acc_ref[0] += gr + hr
        acc_ref[1] += gi + hi
        return carry

    lax.fori_loop(0, modes // 2, backward_two, 0)
    for part in range(2):
        wide = cat([acc_ref[part], jnp.zeros((n, width - n), f32)], 1)
        out_ref[part] = pltpu.roll(wide, col, 1)


def window_gradient(col, rows, probe, meas, consts):
    n = meas.shape[0]
    modes = probe.shape[1]
    vmem = pl.BlockSpec(memory_space=pltpu.VMEM)
    flops = modes * 2 * 4 * 3 * 2 * n**3
    return pl.pallas_call(
        gradient_kernel,
        out_shape=jax.ShapeDtypeStruct(rows.shape, f32),
        in_specs=[pl.BlockSpec(memory_space=pltpu.SMEM)] + [vmem] * 7,
        out_specs=vmem,
        scratch_shapes=[
            pltpu.VMEM((modes, 2, n, n), f32),
            pltpu.VMEM((n, n), f32),
            pltpu.VMEM((2, n, n), f32),
            pltpu.VMEM((2, n, n), f32),
        ],
        cost_estimate=pl.CostEstimate(flops=flops, bytes_accessed=8 * modes * n * n, transcendentals=n * n),
        compiler_params=pltpu.CompilerParams(vmem_limit_bytes=48 * 2**20),
        name="window_gradient",
    )(col, rows, probe, meas, *consts)


def body(object_field, probe_modes, measured, positions):
    strips, group = lax.axis_size("strip"), lax.axis_size("mode")
    stripe_rows, width = object_field.shape[1:]
    n = probe_modes.shape[2]
    local = probe_modes.shape[1]
    slots = positions.shape[1]
    copies = group // slots
    halo = HALO
    s, m = lax.axis_index("strip"), lax.axis_index("mode")
    side = s % 2
    q = m // copies
    mine = (q // 2) == side
    consts = tables(n)
    partner = [(i, i ^ 1) for i in range(strips)]

    def window_of(which):
        upper = jnp.where(which == 0, 2, 1)
        lower = jnp.where(which == 0, 0, 3)
        return jnp.where(q % 2 == 0, upper, lower)

    share = n // strips
    piece = lax.dynamic_slice_in_dim(probe_modes, s * share, share, axis=2)
    pieces = lax.all_gather(piece, ("strip", "mode"))
    pieces = pieces.reshape(strips, group, 2, local, share, n)
    probe = pieces.transpose(2, 1, 3, 0, 4, 5).reshape(2, group * local, n, n)

    below = lax.ppermute(object_field[:, :halo], "strip", [(i + 1, i) for i in range(strips - 1)])
    frame = jnp.concatenate([object_field, below], axis=1)
    own_rows = jnp.where(q % 2 == 0, frame[:, :stripe_rows], frame[:, halo:])
    theirs = lax.ppermute(own_rows, "strip", partner)
    rows = jnp.where(mine, own_rows, theirs)

    pick = lambda which: lax.dynamic_index_in_dim(measured[0], window_of(which), 0, keepdims=False)
    meas = jnp.where(mine, pick(side), lax.ppermute(pick(1 - side), "strip", partner))
    meas = meas.reshape(n // 2, 2, n // 2, 2).transpose(1, 0, 3, 2).reshape(n, n)
    at = lambda which: lax.dynamic_index_in_dim(positions[0, :, 1], window_of(which), 0)
    col = jnp.where(mine, at(side), lax.ppermute(at(1 - side), "strip", partner))

    forth = []
    for i in range(strips):
        for j in range(group):
            if j + copies < group:
                forth.append((i * group + j, i * group + j + copies))
            elif i + 2 < strips:
                forth.append((i * group + j, (i + 2) * group + j + copies - group))
    back = [(b, a) for a, b in forth]
    last = jnp.logical_and(s >= strips - 2, q == slots - 1)
    both = ("strip", "mode")
    cells = stripe_rows * strips * width
    for iteration in range(ITERS):
        mine_grad = window_gradient(col, rows, probe, meas, consts)
        pair = mine_grad + lax.ppermute(mine_grad, "strip", partner)
        from_prev = lax.ppermute(pair[:, halo:], both, forth)
        from_next = lax.ppermute(pair[:, :halo], both, back)
        top = pair[:, :halo] + from_prev
        bottom = jnp.where(last, 0.0, pair[:, halo:] + from_next)
        square_sum = lax.psum(jnp.sum(top * top), both) / (2 * copies)
        factor = step_scale / jnp.sqrt(square_sum / cells + epsilon)
        rows = rows + factor * jnp.concatenate([top, bottom], axis=1)

    part_rows = halo // 2
    mine_part = lax.dynamic_slice_in_dim(rows, side * part_rows, part_rows, axis=1)
    parts = lax.all_gather(mine_part, "mode")[::copies]
    keep = lax.dynamic_slice_in_dim(parts, 2 * side, 2, axis=0)
    give = lax.dynamic_slice_in_dim(parts, 2 * (1 - side), 2, axis=0)
    got = lax.ppermute(give, "strip", partner)
    low = jnp.where(side == 0, keep, got)
    high = jnp.where(side == 0, got, keep)
    whole = jnp.concatenate([low, high], axis=2)
    return whole.transpose(1, 0, 2, 3).reshape(2, stripe_rows, width)


def solution(mesh):
    return jax.shard_map(
        body,
        mesh=mesh,
        in_specs=(
            P(None, "strip", None),
            P(None, "mode", None, None),
            P("strip", None, None, None),
            P("strip", None, None),
        ),
        out_specs=P(None, "strip", None),
        check_vma=False,
    )
```

time: 822 us -> 364 us (0.44); the launches traced: 812 us -> 363 us
  waiting for transfers between devices: 432 us -> 89.8 us
  matrix products: 132 us -> 0 us
  blocking collectives: 54.9 us -> 134 us
  local copies, waits for them, and re-layouts: 102 us -> 43.6 us
  Pallas kernels: 0 us -> 42.6 us
  other arithmetic: 50.7 us -> 11.6 us
  starting transfers between devices: 9.27 us -> 24.9 us
  between operations: 31.3 us -> 16.9 us
    psum x6 -> x0, waiting for transfers between devices: 424 us -> none  [the longest x3 257 us: body(): grad_real, grad_imag = lax.psum((grad_real, grad_imag), 'mode')]
    dot_general x24 -> x0, matrix products: 132 us -> none  [the longest x6 43.8 us: transform(): jnp.einsum('jk,bkl->bjl', stacked_rows, part_imag, precision=highest)]
    dynamic_update_slice x12 -> x0, local copies, waits for them, and re-layouts: 79.7 us -> none  [body(): lax.dynamic_update_slice(frame_grad, current + jnp.stack([grad_real[slot]...]
    ppermute x6 -> x14, waiting for transfers between devices: 7.98 us -> 70.3 us  [the longest x3 37.8 us: body(): from_next = lax.ppermute(pair[:, :halo], both, back)]
    psum x3, blocking collectives: 54.9 us -> 116 us  [body(): square_sum = lax.psum(jnp.sum(top * top), both) / (2 * copies)]
    pallas_call x0 -> x3, Pallas kernels: none -> 42.6 us  [window_gradient(): pl.pallas_call(gradient_kernel, out_shape=jax.ShapeDtypeStruct(rows.shape...]
    reshape x0 -> x2, local copies, waits for them, and re-layouts: none -> 22.9 us  [the longest x1 18.1 us: body(): meas.reshape(n // 2, 2, n // 2, 2).transpose(1, 0, 3, 2).reshape(n, n)]
    all_gather x0 -> x1, waiting for transfers between devices: none -> 19.5 us  [body(): pieces = lax.all_gather(piece, ('strip', 'mode'))]
  transfers between devices with their start and end apart: 12 -> 15, of which waited for: 11 -> 13; matrix products, arithmetic and copies ran while one was open for 1% -> 9% of each run, Pallas kernels for 0% -> 0%
where the time goes in v1:
time: 364 us; the launch traced here: 363 us
  blocking collectives  134 us (37%)
  waiting for transfers between devices  89.8 us (25%)
  local copies, waits for them, and re-layouts  43.6 us (12%)
  Pallas kernels  42.6 us (12%)
  starting transfers between devices  24.9 us (7%)
  between operations  16.9 us (5%)
  other arithmetic  11.6 us (3%)
    psum x3, blocking collectives, body(): square_sum = lax.psum(jnp.sum(top * top), both) / (2 * copies)  116 us
    pallas_call x3, Pallas kernels, window_gradient(): pl.pallas_call(gradient_kernel, out_shape=jax.ShapeDtypeStruct(rows.shape...  42.6 us
    ppermute x3, waiting for transfers between devices, body(): from_next = lax.ppermute(pair[:, :halo], both, back)  37.8 us
    ppermute x3, waiting for transfers between devices, body(): from_prev = lax.ppermute(pair[:, halo:], both, forth)  20.9 us
    all_gather x1, waiting for transfers between devices, body(): pieces = lax.all_gather(piece, ('strip', 'mode'))  19.5 us
    reshape x1, local copies, waits for them, and re-layouts, body(): meas.reshape(n // 2, 2, n // 2, 2).transpose(1, 0, 3, 2).reshape(n, n)  18.1 us
    all_gather x1, blocking collectives, body(): parts = lax.all_gather(mine_part, 'mode')[::copies]  17.9 us
    ppermute x3, starting transfers between devices, body(): from_prev = lax.ppermute(pair[:, halo:], both, forth)  11.7 us
  transfers between devices with their start and end apart: 15, of which 13 were waited for; matrix products, arithmetic and copies ran while one was open for 9% of the time, Pallas kernels for 0%

profile of v1, /device:TPU:0, one launch (start us, length us, event | category | flops | bytes accessed | tf_op | source)
XLA Modules:
  0.0 363.1 jit_solution(5135944240200036150)
XLA Ops:
  6.5 1.2 copy-done
  7.8 0.7 constant_dynamic-slice_fusion.1
  8.4 1.0 slice.34
  9.5 1.3 collective-permute-start
  10.8 2.3 collective-permute-done
  13.1 1.3 fusion
  14.4 6.9 %collective-permute-start.1 = (f32[2,256,384]{2,1,0:T(8,128)S(1)}, f32[2,256,384]{2,1,0:T(8,128)}, u32[]{:S(2)}, u32[]{:S(2)}) collective-permute-start(f32[2,256,384]{2,1,0:T(8,128)S(1)} %fusion), channel_id=1, source_target_pairs={{0,4},{4,0},{8,12},{12,8},{16,20},{20,16},{24,28},{28,24},{1,5},{5... | collective-permute-start | bytes 2359304 | tf_op jit(solution)/shard_map/ppermute | solution.py:202
  21.3 1.0 dynamic-slice_bitcast_fusion
  22.3 0.1 collective-permute-start.3
  22.4 0.7 slice.36
  23.1 0.6 constant_dynamic-slice_fusion.2
  23.7 0.5 collective-permute-start.2
  24.2 1.0 collective-permute-done.2
  26.5 1.0 bitcast_select_fusion
  27.5 18.1 %reshape.24 = f32[128,2,128,2]{3,2,1,0:T(8,128)} reshape(f32[256,256]{1,0:T(8,128)S(1)} %bitcast_select_fusion) | data formatting | bytes 524288 | tf_op jit(solution)/shard_map/reshape | solution.py:207
  45.5 9.5 %copy.17 = f32[2,128,2,128]{3,2,1,0:T(2,128)S(1)} copy(f32[2,128,2,128]{2,3,0,1:T(8,128)} %bitcast.24) | data formatting | bytes 524288 | tf_op jit(solution)/shard_map/transpose | solution.py:207
  55.1 0.2 broadcast_select_fusion.obj_ref
  55.2 19.5 %all-gather.4.cloned.1.call-done = f32[64,2,32,256]{3,2,1,0:T(8,128)} async-done(((f32[2,2,32,256]{3,2,1,0:T(8,128)}), f32[64,2,32,256]{3,2,1,0:T(8,128)}) %all-gather.4.cloned.1.call-update) | async-done | bytes 4194320 | tf_op jit(solution)/shard_map/all_gather | solution.py:195
  74.7 4.8 %copy.16 = f32[8,4,2,2,32,256]{5,4,0,3,1,2:T(8,128)} copy(f32[8,4,2,2,32,256]{5,4,3,2,1,0:T(8,128)} %bitcast.25) | data formatting | bytes 8388608 | tf_op jit(solution)/shard_map/reshape | solution.py:196
  79.6 14.2 %window_gradient.3 = f32[2,256,384]{2,1,0:T(8,128)S(1)} custom-call(s32[1]{0:T(128)S(6)} %select_n.141.col_ref, f32[2,256,384]{2,1,0:T(8,128)S(1)} %broadcast_select_fusion.obj_ref, f32[2,8,256,256]{3,2,1,0:T(8,128)} %bitcast.26, f32[256,256]{1,0:T(8,128)S(1)} %bitcast.21, bf16[4,256,256]{2,1,0:T(8,128)(2,1)S(1)} %copy-done.1, ...), custom_call_target="tpu_custom_call" | custom-call | flops 6442450944 | bytes 4194304 | tf_op jit(solution)/shard_map/window_gradient/pallas_call | solution.py:156
  93.8 0.3 collective-permute-start.4
  94.1 2.0 collective-permute-done.4
  96.1 0.1 add.85
  96.2 1.0 fusion.8
  97.2 4.1 %collective-permute-start.5 = (f32[2,128,384]{2,1,0:T(8,128)}, f32[2,128,384]{2,1,0:T(8,128)}, u32[]{:S(2)}, u32[]{:S(2)}) collective-permute-start(f32[2,128,384]{2,1,0:T(8,128)} %get-tuple-element.20), channel_id=1, source_target_pairs={{0,1},{1,2},{2,3},{3,8},{4,5},{5,6},{6,7},{7,12},{8,9},{9,10},{10,... | collective-permute-start | bytes 1179656 | tf_op jit(solution)/shard_map/ppermute | solution.py:225
  101.3 1.3 collective-permute-start.6
  102.6 7.0 %collective-permute-done.5 = f32[2,128,384]{2,1,0:T(8,128)} collective-permute-done((f32[2,128,384]{2,1,0:T(8,128)}, f32[2,128,384]{2,1,0:T(8,128)}, u32[]{:S(2)}, u32[]{:S(2)}) %collective-permute-start.5) | collective-permute-done | bytes 393248 | tf_op jit(solution)/shard_map/ppermute | solution.py:225
  109.6 12.0 %collective-permute-done.6 = f32[2,128,384]{2,1,0:T(8,128)} collective-permute-done((f32[2,128,384]{2,1,0:T(8,128)}, f32[2,128,384]{2,1,0:T(8,128)}, u32[]{:S(2)}, u32[]{:S(2)}) %collective-permute-start.6) | collective-permute-done | bytes 393248 | tf_op jit(solution)/shard_map/ppermute | solution.py:226
  121.6 2.8 multiply_reduce_fusion.2
  124.4 38.3 %psum.21 = f32[]{:T(128)} all-reduce(f32[]{:T(128)} %get-tuple-element.9), channel_id=1, replica_groups=mesh['strip'=8,'mode'=4] {'strip','mode'}, use_global_device_ids=true, to_apply=%region_1.2 | all-reduce | flops 1 | bytes 8 | tf_op jit(solution)/shard_map/psum | solution.py:229
  163.4 1.2 fusion.1.obj_ref
  164.6 1.0 copy-done.3
  165.7 0.9 copy-done.6
  166.6 14.3 %window_gradient.4 = f32[2,256,384]{2,1,0:T(8,128)S(1)} custom-call(s32[1]{0:T(128)S(6)} %select_n.141.col_ref, f32[2,256,384]{2,1,0:T(8,128)S(1)} %fusion.1.obj_ref, f32[2,8,256,256]{3,2,1,0:T(8,128)} %bitcast.27, f32[256,256]{1,0:T(8,128)S(1)} %bitcast.22, bf16[4,256,256]{2,1,0:T(8,128)(2,1)S(1)} %copy-done.1, bf16[2,512,256]{2,1,0:T(8,128)(2,1)S(1)} %copy-done.3, ...), custom_call_target="tpu_custom_call" | custom-call | flops 6442450944 | bytes 4194304 | tf_op jit(solution)/shard_map/window_gradient/pallas_call | solution.py:156
  180.9 0.1 collective-permute-start.7
  181.0 2.3 collective-permute-done.7
  183.2 0.1 add.90
  183.3 0.1 fusion.7
  183.4 3.5 collective-permute-start.8
  186.9 1.3 collective-permute-start.9
  188.2 7.3 %collective-permute-done.8 = f32[2,128,384]{2,1,0:T(8,128)S(1)} collective-permute-done((f32[2,128,384]{2,1,0:T(8,128)S(1)}, f32[2,128,384]{2,1,0:T(8,128)S(1)}, u32[]{:S(2)}, u32[]{:S(2)}) %collective-permute-start.8) | collective-permute-done | bytes 393248 | tf_op jit(solution)/shard_map/ppermute | solution.py:225
  195.5 12.6 %collective-permute-done.9 = f32[2,128,384]{2,1,0:T(8,128)S(1)} collective-permute-done((f32[2,128,384]{2,1,0:T(8,128)S(1)}, f32[2,128,384]{2,1,0:T(8,128)S(1)}, u32[]{:S(2)}, u32[]{:S(2)}) %collective-permute-start.9) | collective-permute-done | bytes 393248 | tf_op jit(solution)/shard_map/ppermute | solution.py:226
  208.1 1.7 multiply_reduce_fusion.1
  209.8 38.9 %psum.22 = f32[]{:T(128)} all-reduce(f32[]{:T(128)} %get-tuple-element.7), channel_id=1, replica_groups=mesh['strip'=8,'mode'=4] {'strip','mode'}, use_global_device_ids=true, to_apply=%region_3.4 | all-reduce | flops 1 | bytes 8 | tf_op jit(solution)/shard_map/psum | solution.py:229
  249.3 1.2 fusion.2.obj_ref
  250.6 1.0 copy-done.4
  251.6 0.9 copy-done.7
  252.5 14.2 %window_gradient.5 = f32[2,256,384]{2,1,0:T(8,128)S(1)} custom-call(s32[1]{0:T(128)S(6)} %select_n.141.col_ref, f32[2,256,384]{2,1,0:T(8,128)S(1)} %fusion.2.obj_ref, f32[2,8,256,256]{3,2,1,0:T(8,128)} %bitcast.28, f32[256,256]{1,0:T(8,128)S(1)} %bitcast.23, bf16[4,256,256]{2,1,0:T(8,128)(2,1)S(1)} %copy-done.1, bf16[2,512,256]{2,1,0:T(8,128)(2,1)S(1)} %copy-done.4, ...), custom_call_target="tpu_custom_call" | custom-call | flops 6442450944 | bytes 4194304 | tf_op jit(solution)/shard_map/window_gradient/pallas_call | solution.py:156
  266.7 0.1 collective-permute-start.10
  266.8 2.3 collective-permute-done.10
  269.1 0.1 add.95
  269.2 0.1 fusion.6
  269.2 4.1 %collective-permute-start.11 = (f32[2,128,384]{2,1,0:T(8,128)S(1)}, f32[2,128,384]{2,1,0:T(8,128)}, u32[]{:S(2)}, u32[]{:S(2)}) collective-permute-start(f32[2,128,384]{2,1,0:T(8,128)S(1)} %get-tuple-element.15), channel_id=1, source_target_pairs={{0,1},{1,2},{2,3},{3,8},{4,5},{5,6},{6,7},{7,12},{8,9},{9,10},{10,... | collective-permute-start | bytes 1179656 | tf_op jit(solution)/shard_map/ppermute | solution.py:225
  273.3 1.3 collective-permute-start.12
  274.6 6.6 %collective-permute-done.11 = f32[2,128,384]{2,1,0:T(8,128)} collective-permute-done((f32[2,128,384]{2,1,0:T(8,128)S(1)}, f32[2,128,384]{2,1,0:T(8,128)}, u32[]{:S(2)}, u32[]{:S(2)}) %collective-permute-start.11) | collective-permute-done | bytes 393248 | tf_op jit(solution)/shard_map/ppermute | solution.py:225
  281.2 13.2 %collective-permute-done.12 = f32[2,128,384]{2,1,0:T(8,128)} collective-permute-done((f32[2,128,384]{2,1,0:T(8,128)S(1)}, f32[2,128,384]{2,1,0:T(8,128)}, u32[]{:S(2)}, u32[]{:S(2)}) %collective-permute-start.12) | collective-permute-done | bytes 393248 | tf_op jit(solution)/shard_map/ppermute | solution.py:226
  294.4 1.8 multiply_reduce_fusion
  296.2 38.5 %psum.23 = f32[]{:T(128)} all-reduce(f32[]{:T(128)} %get-tuple-element.5), channel_id=1, replica_groups=mesh['strip'=8,'mode'=4] {'strip','mode'}, use_global_device_ids=true, to_apply=%region_5.6 | all-reduce | flops 1 | bytes 8 | tf_op jit(solution)/shard_map/psum | solution.py:229
  335.4 0.1 fusion.5
  335.5 17.9 %all-gather.1 = f32[8,64,384]{2,1,0:T(8,128)S(1)} all-gather(f32[2,64,384]{2,1,0:T(8,128)S(1)} %fusion.5), channel_id=3, replica_groups=mesh['strip'=8,'mode'=4] {'mode'}, dimensions={0}, use_global_device_ids=true | all-gather | bytes 983040 | tf_op jit(solution)/shard_map/all_gather | solution.py:235
  353.4 0.1 collective-permute-start.13
  353.5 1.7 collective-permute-done.13
  355.2 0.1 dynamic-slice_select_fusion.1
  355.4 0.9 copy.18
  (20 shorter events, 0.2 us)
Async XLA Ops:
  6.5 1.2 copy-start
  6.5 68.2 %all-gather.4.cloned.1.call-start = ((), (), s32[]{:S(2)}) async-start(), calls=%async_computation | async-start | bytes 4325376 | tf_op jit(solution)/shard_map/all_gather | solution.py:195
  9.5 3.6 collective-permute-start
  14.4 40.6 %collective-permute-start.1 = (f32[2,256,384]{2,1,0:T(8,128)S(1)}, f32[2,256,384]{2,1,0:T(8,128)}, u32[]{:S(2)}, u32[]{:S(2)}) collective-permute-start(f32[2,256,384]{2,1,0:T(8,128)S(1)} %fusion), channel_id=1, source_target_pairs={{0,4},{4,0},{8,12},{12,8},{16,20},{20,16},{24,28},{28,24},{1,5},{5... | collective-permute-start | bytes 2359304 | tf_op jit(solution)/shard_map/ppermute | solution.py:202
  22.3 4.1 %collective-permute-start.3 = (f32[256,256]{1,0:T(8,128)S(1)}, f32[256,256]{1,0:T(8,128)S(1)}, u32[]{:S(2)}, u32[]{:S(2)}) collective-permute-start(f32[256,256]{1,0:T(8,128)S(1)} %dynamic-slice_bitcast_fusion), channel_id=1, source_target_pairs={{0,4},{4,0},{8,12},{12,8},{16,20},{20,16},{24,28},{28,24},{1,5},{5... | collective-permute-start | bytes 786440 | tf_op jit(solution)/shard_map/ppermute | solution.py:206
  23.7 1.5 collective-permute-start.2
  74.7 4.9 %copy-start.1 = (bf16[4,256,256]{2,1,0:T(8,128)(2,1)S(1)}, bf16[4,256,256]{2,1,0:T(8,128)(2,1)}, u32[]{:S(2)}) copy-start(bf16[4,256,256]{2,1,0:T(8,128)(2,1)} %constant.130.rights) | copy-start | bytes 1572868
  74.7 4.9 %copy-start.2 = (bf16[2,512,256]{2,1,0:T(8,128)(2,1)S(1)}, bf16[2,512,256]{2,1,0:T(8,128)(2,1)}, u32[]{:S(2)}) copy-start(bf16[2,512,256]{2,1,0:T(8,128)(2,1)} %constant.135.lefts) | copy-start | bytes 1572868
  74.7 4.9 %copy-start.5 = (f32[2,128,256]{2,1,0:T(8,128)S(1)}, f32[2,128,256]{2,1,0:T(8,128)}, u32[]{:S(2)}) copy-start(f32[2,128,256]{2,1,0:T(8,128)} %constant.114.clone.subs) | copy-start | bytes 786436
  74.7 4.9 %copy-start.8 = (f32[2,1,128]{2,1,0:T(1,128)S(1)}, f32[2,1,128]{2,1,0:T(1,128)}, u32[]{:S(2)}) copy-start(f32[2,1,128]{2,1,0:T(1,128)} %constant.136.lanes) | copy-start | bytes 3076
  93.8 2.4 collective-permute-start.4
  97.2 12.4 %collective-permute-start.5 = (f32[2,128,384]{2,1,0:T(8,128)}, f32[2,128,384]{2,1,0:T(8,128)}, u32[]{:S(2)}, u32[]{:S(2)}) collective-permute-start(f32[2,128,384]{2,1,0:T(8,128)} %get-tuple-element.20), channel_id=1, source_target_pairs={{0,1},{1,2},{2,3},{3,8},{4,5},{5,6},{6,7},{7,12},{8,9},{9,10},{10,... | collective-permute-start | bytes 1179656 | tf_op jit(solution)/shard_map/ppermute | solution.py:225
  101.3 20.3 %collective-permute-start.6 = (f32[2,128,384]{2,1,0:T(8,128)}, f32[2,128,384]{2,1,0:T(8,128)}, u32[]{:S(2)}, u32[]{:S(2)}) collective-permute-start(f32[2,128,384]{2,1,0:T(8,128)} %get-tuple-element.21), channel_id=1, source_target_pairs={{1,0},{2,1},{3,2},{8,3},{5,4},{6,5},{7,6},{12,7},{9,8},{10,9},{11,... | collective-permute-start | bytes 1179656 | tf_op jit(solution)/shard_map/ppermute | solution.py:226
  164.6 1.0 copy-start.3
  165.7 0.9 copy-start.6
  180.9 2.4 collective-permute-start.7
  183.4 12.2 %collective-permute-start.8 = (f32[2,128,384]{2,1,0:T(8,128)S(1)}, f32[2,128,384]{2,1,0:T(8,128)S(1)}, u32[]{:S(2)}, u32[]{:S(2)}) collective-permute-start(f32[2,128,384]{2,1,0:T(8,128)S(1)} %get-tuple-element.17), channel_id=1, source_target_pairs={{0,1},{1,2},{2,3},{3,8},{4,5},{5,6},{6,7},{7,12},{8,9},{9,10},{10,... | collective-permute-start | bytes 1179656 | tf_op jit(solution)/shard_map/ppermute | solution.py:225
  186.9 21.2 %collective-permute-start.9 = (f32[2,128,384]{2,1,0:T(8,128)S(1)}, f32[2,128,384]{2,1,0:T(8,128)S(1)}, u32[]{:S(2)}, u32[]{:S(2)}) collective-permute-start(f32[2,128,384]{2,1,0:T(8,128)S(1)} %get-tuple-element.18), channel_id=1, source_target_pairs={{1,0},{2,1},{3,2},{8,3},{5,4},{6,5},{7,6},{12,7},{9,8},{10,9},{11,... | collective-permute-start | bytes 1179656 | tf_op jit(solution)/shard_map/ppermute | solution.py:226
  250.5 1.0 copy-start.4
  251.6 0.9 copy-start.7
  266.7 2.4 collective-permute-start.10
  269.2 12.0 %collective-permute-start.11 = (f32[2,128,384]{2,1,0:T(8,128)S(1)}, f32[2,128,384]{2,1,0:T(8,128)}, u32[]{:S(2)}, u32[]{:S(2)}) collective-permute-start(f32[2,128,384]{2,1,0:T(8,128)S(1)} %get-tuple-element.15), channel_id=1, source_target_pairs={{0,1},{1,2},{2,3},{3,8},{4,5},{5,6},{6,7},{7,12},{8,9},{9,10},{10,... | collective-permute-start | bytes 1179656 | tf_op jit(solution)/shard_map/ppermute | solution.py:225
  273.3 21.1 %collective-permute-start.12 = (f32[2,128,384]{2,1,0:T(8,128)S(1)}, f32[2,128,384]{2,1,0:T(8,128)}, u32[]{:S(2)}, u32[]{:S(2)}) collective-permute-start(f32[2,128,384]{2,1,0:T(8,128)S(1)} %get-tuple-element.14), channel_id=1, source_target_pairs={{1,0},{2,1},{3,2},{8,3},{5,4},{6,5},{7,6},{12,7},{9,8},{10,9},{11,... | collective-permute-start | bytes 1179656 | tf_op jit(solution)/shard_map/ppermute | solution.py:226
  353.4 1.8 collective-permute-start.13
Sparse Core Ops, SparseCore 0:
  10.3 64.3 all-gather.3

commit v2 on v1

--- a/solution.py
+++ b/solution.py
@@ -16,6 +16,7 @@
 epsilon = 1e-06
 f32 = jnp.float32
 bf16 = jnp.bfloat16
+MESH = pl.DeviceIdType.MESH
 
 
 def tables(n):
@@ -170,6 +171,160 @@
     )(col, rows, probe, meas, *consts)
 
 
+def exchange_kernel(copies, slots, cells, g_ref, rows_ref, out_ref, pair, from_partner, from_prev, from_next, own, other, tile, tiles_a, sum_a, tiles_b, partner_sems, chain_sems, back_sems, a_send, a_recv, b_send, b_recv):
+    strips, group = lax.axis_size("strip"), lax.axis_size("mode")
+    s, m = lax.axis_index("strip"), lax.axis_index("mode")
+    h, q = s % 2, m // copies
+    width = g_ref.shape[-1]
+    partner = (s + 1 - 2 * h, m)
+    inner_next, inner_prev = q < slots - 1, q > 0
+    has_next = jnp.logical_or(inner_next, s < strips - 2)
+    has_prev = jnp.logical_or(inner_prev, s >= 2)
+    cross = (slots - 1) * copies
+    after = (jnp.where(inner_next, s, s + 2), jnp.where(inner_next, m + copies, m - cross))
+    before = (jnp.where(inner_prev, s, s - 2), jnp.where(inner_prev, m - copies, m + cross))
+    cross_next = jnp.logical_and(has_next, jnp.logical_not(inner_next))
+    cross_prev = jnp.logical_and(has_prev, jnp.logical_not(inner_prev))
+
+    barrier = pltpu.get_barrier_semaphore()
+
+    def greet(device):
+        pl.semaphore_signal(barrier, inc=1, device_id=device, device_id_type=MESH)
+
+    for d in range(1, group):
+        greet((s, (m + d) % group))
+    for d in range(1, strips):
+        greet(((s + d) % strips, m))
+
+    @pl.when(cross_next)
+    def _():
+        greet(after)
+
+    @pl.when(cross_prev)
+    def _():
+        greet(before)
+
+    extra = jnp.where(cross_next, 1, 0) + jnp.where(cross_prev, 1, 0)
+    pl.semaphore_wait(barrier, group + strips - 2 + extra)
+
+    def send(src, dst, send_sem, recv_sem, device):
+        return pltpu.make_async_remote_copy(
+            src_ref=src, dst_ref=dst, send_sem=send_sem, recv_sem=recv_sem,
+            device_id=device, device_id_type=MESH,
+        )
+
+    first = send(g_ref.at[:, :, 1 - h], from_partner, partner_sems.at[0], partner_sems.at[1], partner)
+    first.start()
+    first.wait()
+    pair[...] = g_ref[:, :, h] + from_partner[...]
+    down = send(pair.at[:, 1], from_prev, chain_sems.at[0], chain_sems.at[1], after)
+    up = send(pair.at[:, 0], from_next, chain_sems.at[2], chain_sems.at[3], before)
+
+    @pl.when(has_next)
+    def _():
+        down.start()
+
+    @pl.when(has_prev)
+    def _():
+        up.start()
+
+    @pl.when(has_prev)
+    def _():
+        down.wait_recv()
+        own[:, 0] = pair[:, 0] + from_prev[...]
+
+    @pl.when(jnp.logical_not(has_prev))
+    def _():
+        own[:, 0] = pair[:, 0]
+
+    top = own[:, 0]
+    squares = jnp.sum(top * top, axis=0)
+    squares = jnp.sum(squares.reshape(-1, 8, width), axis=0)
+    folded = squares[:, :128]
+    for lane in range(128, width, 128):
+        folded = folded + squares[:, lane : lane + 128]
+    tile[...] = folded
+    sends_a = [
+        send(tile, tiles_a.at[d - 1], a_send.at[d - 1], a_recv.at[d - 1], (s, (m + d) % group))
+        for d in range(1, group)
+    ]
+    for copy in sends_a:
+        copy.start()
+
+    @pl.when(has_next)
+    def _():
+        up.wait_recv()
+        own[:, 1] = pair[:, 1] + from_next[...]
+
+    @pl.when(jnp.logical_not(has_next))
+    def _():
+        own[:, 1] = jnp.zeros_like(from_next)
+
+    second = send(own, other, back_sems.at[0], back_sems.at[1], partner)
+    second.start()
+
+    total = tile[...]
+    for d in range(1, group):
+        sends_a[d - 1].wait_recv()
+        total = total + tiles_a[d - 1]
+    sum_a[...] = total
+    sends_b = [
+        send(sum_a, tiles_b.at[d - 1], b_send.at[d - 1], b_recv.at[d - 1], ((s + d) % strips, m))
+        for d in range(1, strips)
+    ]
+    for copy in sends_b:
+        copy.start()
+    second.wait_recv()
+    for d in range(1, strips):
+        sends_b[d - 1].wait_recv()
+        total = total + tiles_b[d - 1]
+    total = jnp.sum(jnp.sum(total, axis=1, keepdims=True), axis=0, keepdims=True)
+    factor = step_scale / jnp.sqrt(total / (cells * copies) + epsilon)
+    factor = factor.reshape(1, 1, 1, 1)
+    out_ref[:, :, h] = rows_ref[:, :, h] + factor * own[...]
+    out_ref[:, :, 1 - h] = rows_ref[:, :, 1 - h] + factor * other[...]
+
+    @pl.when(has_next)
+    def _():
+        down.wait_send()
+
+    @pl.when(has_prev)
+    def _():
+        up.wait_send()
+
+    for copy in sends_a + [second] + sends_b:
+        copy.wait_send()
+
+
+def exchange(grad, rows, copies, slots, cells):
+    strips, group = lax.axis_size("strip"), lax.axis_size("mode")
+    parts, total_rows, width = rows.shape
+    quarter = total_rows // 4
+    shape = (parts, 2, 2, quarter, width)
+    vmem = pl.BlockSpec(memory_space=pltpu.VMEM)
+    mine = pltpu.VMEM((parts, 2, quarter, width), f32)
+    piece = pltpu.VMEM((parts, quarter, width), f32)
+    dma = pltpu.SemaphoreType.DMA
+    out = pl.pallas_call(
+        functools.partial(exchange_kernel, copies, slots, float(cells)),
+        out_shape=jax.ShapeDtypeStruct(shape, f32),
+        in_specs=[vmem, vmem],
+        out_specs=vmem,
+        scratch_shapes=[
+            mine, mine, piece, piece, mine, mine,
+            pltpu.VMEM((8, 128), f32),
+            pltpu.VMEM((group - 1, 8, 128), f32),
+            pltpu.VMEM((8, 128), f32),
+            pltpu.VMEM((strips - 1, 8, 128), f32),
+            dma((2,)), dma((4,)), dma((2,)),
+            dma((group - 1,)), dma((group - 1,)), dma((strips - 1,)), dma((strips - 1,)),
+        ],
+        compiler_params=pltpu.CompilerParams(collective_id=0, has_side_effects=True, vmem_limit_bytes=32 * 2**20),
+        name="exchange",
+    )(grad.reshape(shape), rows.reshape(shape))
+    return out.reshape(rows.shape)
+
+
 def body(object_field, probe_modes, measured, positions):
     strips, group = lax.axis_size("strip"), lax.axis_size("mode")
     stripe_rows, width = object_field.shape[1:]
@@ -208,27 +363,10 @@
     at = lambda which: lax.dynamic_index_in_dim(positions[0, :, 1], window_of(which), 0)
     col = jnp.where(mine, at(side), lax.ppermute(at(1 - side), "strip", partner))
 
-    forth = []
-    for i in range(strips):
-        for j in range(group):
-            if j + copies < group:
-                forth.append((i * group + j, i * group + j + copies))
-            elif i + 2 < strips:
-                forth.append((i * group + j, (i + 2) * group + j + copies - group))
-    back = [(b, a) for a, b in forth]
-    last = jnp.logical_and(s >= strips - 2, q == slots - 1)
-    both = ("strip", "mode")
     cells = stripe_rows * strips * width
     for iteration in range(ITERS):
-        mine_grad = window_gradient(col, rows, probe, meas, consts)
-        pair = mine_grad + lax.ppermute(mine_grad, "strip", partner)
-        from_prev = lax.ppermute(pair[:, halo:], both, forth)
-        from_next = lax.ppermute(pair[:, :halo], both, back)
-        top = pair[:, :halo] + from_prev
-        bottom = jnp.where(last, 0.0, pair[:, halo:] + from_next)
-        square_sum = lax.psum(jnp.sum(top * top), both) / (2 * copies)
-        factor = step_scale / jnp.sqrt(square_sum / cells + epsilon)
-        rows = rows + factor * jnp.concatenate([top, bottom], axis=1)
+        grad = window_gradient(col, rows, probe, meas, consts)
+        rows = exchange(grad, rows, copies, slots, cells)
 
     part_rows = halo // 2
     mine_part = lax.dynamic_slice_in_dim(rows, side * part_rows, part_rows, axis=1)

time: 364 us -> 212 us (0.58)
  blocking collectives: 134 us -> 19.9 us
  waiting for transfers between devices: 89.8 us -> 24.5 us
  Pallas kernels: 42.6 us -> 102 us
  starting transfers between devices: 24.9 us -> 8.85 us
  other arithmetic: 11.6 us -> 2.53 us
  local copies, waits for them, and re-layouts: 43.6 us -> 38.6 us
    psum x3 -> x0, blocking collectives: 116 us -> none  [body(): square_sum = lax.psum(jnp.sum(top * top), both) / (2 * copies)]
    ppermute x9 -> x0, waiting for transfers between devices: 65.3 us -> none  [the longest x3 37.8 us: body(): from_next = lax.ppermute(pair[:, :halo], both, back)]
    pallas_call x0 -> x3, Pallas kernels: none -> 59.4 us  [exchange(): pl.pallas_call(functools.partial(exchange_kernel, copies, slots, float(ce...]
    ppermute x9 -> x0, starting transfers between devices: 16 us -> none  [the longest x3 11.7 us: body(): from_prev = lax.ppermute(pair[:, halo:], both, forth)]
    reduce_sum x3 -> x0, other arithmetic: 6.27 us -> none  [body(): square_sum = lax.psum(jnp.sum(top * top), both) / (2 * copies)]
    unnamed x19 -> x11, local copies, waits for them, and re-layouts: 5.23 us -> 1.26 us
  transfers between devices with their start and end apart: 15 -> 6, of which waited for: 13 -> 4; matrix products, arithmetic and copies ran while one was open for 9% -> 16% of each run, Pallas kernels for 0% -> 0%
where the time goes in v2:
time: 212 us; the launch traced here: 211 us
  Pallas kernels  102 us (48%)
  local copies, waits for them, and re-layouts  38.6 us (18%)
  waiting for transfers between devices  24.5 us (12%)
  blocking collectives  19.9 us (9%)
  between operations  14.8 us (7%)
  starting transfers between devices  8.85 us (4%)
  other arithmetic  2.53 us (1%)
    pallas_call x3, Pallas kernels, exchange(): pl.pallas_call(functools.partial(exchange_kernel, copies, slots, float(ce...  59.4 us
    pallas_call x3, Pallas kernels, window_gradient(): pl.pallas_call(gradient_kernel, out_shape=jax.ShapeDtypeStruct(rows.shape...  42.5 us
    all_gather x1, blocking collectives, body(): parts = lax.all_gather(mine_part, 'mode')[::copies]  19.9 us
    all_gather x1, waiting for transfers between devices, body(): pieces = lax.all_gather(piece, ('strip', 'mode'))  19.5 us
    reshape x1, local copies, waits for them, and re-layouts, body(): meas.reshape(n // 2, 2, n // 2, 2).transpose(1, 0, 3, 2).reshape(n, n)  18.1 us
    transpose x1, local copies, waits for them, and re-layouts, body(): meas.reshape(n // 2, 2, n // 2, 2).transpose(1, 0, 3, 2).reshape(n, n)  9.5 us
    ppermute x1, starting transfers between devices, body(): theirs = lax.ppermute(own_rows, 'strip', partner)  6.91 us
    reshape x1, local copies, waits for them, and re-layouts, body(): pieces = pieces.reshape(strips, group, 2, local, share, n)  4.83 us
  transfers between devices with their start and end apart: 6, of which 4 were waited for; matrix products, arithmetic and copies ran while one was open for 16% of the time, Pallas kernels for 0%

profile of v2, /device:TPU:0, one launch (start us, length us, event | category | flops | bytes accessed | tf_op | source)
XLA Modules:
  0.0 211.2 jit_solution(4017488541906094)
XLA Ops:
  6.5 0.0 copy-start
  6.5 0.0 all-gather.4.cloned.1.call-start
  6.5 1.2 copy-done
  7.8 0.7 constant_dynamic-slice_fusion.2
  8.4 0.0 all-gather.4.cloned.1.call-update
  8.4 1.0 slice.11
  9.5 1.3 collective-permute-start.1
  10.8 2.3 %collective-permute-done.1 = f32[2,128,384]{2,1,0:T(8,128)S(1)} collective-permute-done((f32[2,128,384]{2,1,0:T(8,128)S(1)}, f32[2,128,384]{2,1,0:T(8,128)S(1)}, u32[]{:S(2)}, u32[]{:S(2)}) %collective-permute-start.1) | collective-permute-done | bytes 393248 | tf_op jit(solution)/shard_map/ppermute | solution.py:354
  13.1 1.3 fusion
  14.4 6.9 %collective-permute-start.2 = (f32[2,256,384]{2,1,0:T(8,128)S(1)}, f32[2,256,384]{2,1,0:T(8,128)}, u32[]{:S(2)}, u32[]{:S(2)}) collective-permute-start(f32[2,256,384]{2,1,0:T(8,128)S(1)} %fusion), channel_id=1, source_target_pairs={{0,4},{4,0},{8,12},{12,8},{16,20},{20,16},{24,28},{28,24},{1,5},{5... | collective-permute-start | bytes 2359304 | tf_op jit(solution)/shard_map/ppermute | solution.py:357
  21.3 1.0 dynamic-slice_bitcast_fusion
  22.3 0.1 collective-permute-start.3
  22.4 0.7 slice.10
  23.1 0.6 constant_dynamic-slice_fusion.3
  23.8 0.5 collective-permute-start
  24.2 1.0 collective-permute-done
  26.5 0.0 collective-permute-done.3
  26.5 1.0 bitcast_select_fusion
  27.5 18.1 %reshape.45 = f32[128,2,128,2]{3,2,1,0:T(8,128)} reshape(f32[256,256]{1,0:T(8,128)S(1)} %bitcast_select_fusion) | data formatting | bytes 524288 | tf_op jit(solution)/shard_map/reshape | solution.py:362
  45.6 9.5 %copy.19 = f32[2,128,2,128]{3,2,1,0:T(2,128)S(1)} copy(f32[2,128,2,128]{2,3,0,1:T(8,128)} %bitcast.38) | data formatting | bytes 524288 | tf_op jit(solution)/shard_map/transpose | solution.py:362
  55.1 0.0 collective-permute-done.2
  55.1 0.1 broadcast_select_fusion.obj_ref
  55.2 19.5 %all-gather.4.cloned.1.call-done = f32[64,2,32,256]{3,2,1,0:T(8,128)} async-done(((f32[2,2,32,256]{3,2,1,0:T(8,128)}), f32[64,2,32,256]{3,2,1,0:T(8,128)}) %all-gather.4.cloned.1.call-update) | async-done | bytes 4194320 | tf_op jit(solution)/shard_map/all_gather | solution.py:350
  74.7 0.0 copy-start.1
  74.7 0.0 copy-start.2
  74.7 0.0 copy-start.3
  74.7 0.0 copy-start.4
  74.7 4.8 %copy.18 = f32[8,4,2,2,32,256]{5,4,0,3,1,2:T(8,128)} copy(f32[8,4,2,2,32,256]{5,4,3,2,1,0:T(8,128)} %bitcast.39) | data formatting | bytes 8388608 | tf_op jit(solution)/shard_map/reshape | solution.py:351
  79.6 0.0 copy-done.1
  79.6 0.0 copy-done.2
  79.6 0.0 copy-done.3
  79.6 0.0 copy-done.4
  79.6 14.2 %window_gradient.3 = f32[2,256,384]{2,1,0:T(8,128)S(1)} custom-call(s32[1]{0:T(128)S(6)} %select_n.121.col_ref, f32[2,256,384]{2,1,0:T(8,128)S(1)} %broadcast_select_fusion.obj_ref, f32[2,8,256,256]{3,2,1,0:T(8,128)} %bitcast.40, f32[256,256]{1,0:T(8,128)S(1)} %bitcast.35, bf16[4,256,256]{2,1,0:T(8,128)(2,1)S(1)} %copy-done.1, ...), custom_call_target="tpu_custom_call" | custom-call | flops 6442450944 | bytes 4194304 | tf_op jit(solution)/shard_map/window_gradient/pallas_call | solution.py:157
  93.7 19.8 %exchange.3.rows_ref = f32[2,2,2,64,384]{4,3,2,1,0:T(8,128)S(1)} custom-call(f32[2,2,2,64,384]{4,3,2,1,0:T(8,128)S(1)} %bitcast.33, f32[2,2,2,64,384]{4,3,2,1,0:T(8,128)S(1)} %bitcast.28), custom_call_target="tpu_custom_call" | custom-call | tf_op jit(solution)/shard_map/exchange/pallas_call | solution.py:308
  113.5 14.2 %window_gradient.4 = f32[2,256,384]{2,1,0:T(8,128)S(1)} custom-call(s32[1]{0:T(128)S(6)} %select_n.121.col_ref, f32[2,256,384]{2,1,0:T(8,128)S(1)} %bitcast.30, f32[2,8,256,256]{3,2,1,0:T(8,128)} %bitcast.41, f32[256,256]{1,0:T(8,128)S(1)} %bitcast.36, bf16[4,256,256]{2,1,0:T(8,128)(2,1)S(1)} %copy-done.1, bf16[2,512,256]{2,1,0:T(8,128)(2,1)S(1)} %copy-done.2, ...), custom_call_target="tpu_custom_call" | custom-call | flops 6442450944 | bytes 4194304 | tf_op jit(solution)/shard_map/window_gradient/pallas_call | solution.py:157
  127.7 19.7 %exchange.4.rows_ref = f32[2,2,2,64,384]{4,3,2,1,0:T(8,128)S(1)} custom-call(f32[2,2,2,64,384]{4,3,2,1,0:T(8,128)S(1)} %bitcast.34, f32[2,2,2,64,384]{4,3,2,1,0:T(8,128)S(1)} %exchange.3.rows_ref), custom_call_target="tpu_custom_call" | custom-call | tf_op jit(solution)/shard_map/exchange/pallas_call | solution.py:308
  147.4 14.2 %window_gradient.5 = f32[2,256,384]{2,1,0:T(8,128)S(1)} custom-call(s32[1]{0:T(128)S(6)} %select_n.121.col_ref, f32[2,256,384]{2,1,0:T(8,128)S(1)} %bitcast.29, f32[2,8,256,256]{3,2,1,0:T(8,128)} %bitcast.42, f32[256,256]{1,0:T(8,128)S(1)} %bitcast.37, bf16[4,256,256]{2,1,0:T(8,128)(2,1)S(1)} %copy-done.1, bf16[2,512,256]{2,1,0:T(8,128)(2,1)S(1)} %copy-done.2, ...), custom_call_target="tpu_custom_call" | custom-call | flops 6442450944 | bytes 4194304 | tf_op jit(solution)/shard_map/window_gradient/pallas_call | solution.py:157
  161.6 19.9 %exchange.5 = f32[2,2,2,64,384]{4,3,2,1,0:T(8,128)S(1)} custom-call(f32[2,2,2,64,384]{4,3,2,1,0:T(8,128)S(1)} %bitcast.32, f32[2,2,2,64,384]{4,3,2,1,0:T(8,128)S(1)} %exchange.4.rows_ref), custom_call_target="tpu_custom_call" | custom-call | tf_op jit(solution)/shard_map/exchange/pallas_call | solution.py:308
  181.6 19.9 %all-gather.1 = f32[8,64,384]{2,1,0:T(8,128)S(1)} all-gather(f32[2,64,384]{2,1,0:T(8,128)S(1)} %constant_dynamic-slice_fusion.1), channel_id=3, replica_groups=mesh['strip'=8,'mode'=4] {'mode'}, dimensions={0}, use_global_device_ids=true | all-gather | bytes 983040 | tf_op jit(solution)/shard_map/all_gather | solution.py:373
  201.6 0.1 collective-permute-start.4
  201.6 1.7 collective-permute-done.4
  203.3 0.1 dynamic-slice_select_fusion.1
  203.4 0.1 maximum_bitcast_fusion
  203.5 0.9 copy.20
  (3 shorter events, 0.1 us)
Async XLA Ops:
  6.5 1.2 copy-start
  6.5 68.2 %all-gather.4.cloned.1.call-start = ((), (), s32[]{:S(2)}) async-start(), calls=%async_computation | async-start | bytes 4325376 | tf_op jit(solution)/shard_map/all_gather | solution.py:350
  9.5 3.6 %collective-permute-start.1 = (f32[2,128,384]{2,1,0:T(8,128)S(1)}, f32[2,128,384]{2,1,0:T(8,128)S(1)}, u32[]{:S(2)}, u32[]{:S(2)}) collective-permute-start(f32[2,128,384]{2,1,0:T(8,128)S(1)} %slice.11), channel_id=1, source_target_pairs={{4,0},{8,4},{12,8},{16,12},{20,16},{24,20},{28,24},{5,1},{9,5},{13... | collective-permute-start | bytes 1179656 | tf_op jit(solution)/shard_map/ppermute | solution.py:354
  14.4 40.7 %collective-permute-start.2 = (f32[2,256,384]{2,1,0:T(8,128)S(1)}, f32[2,256,384]{2,1,0:T(8,128)}, u32[]{:S(2)}, u32[]{:S(2)}) collective-permute-start(f32[2,256,384]{2,1,0:T(8,128)S(1)} %fusion), channel_id=1, source_target_pairs={{0,4},{4,0},{8,12},{12,8},{16,20},{20,16},{24,28},{28,24},{1,5},{5... | collective-permute-start | bytes 2359304 | tf_op jit(solution)/shard_map/ppermute | solution.py:357
  22.3 4.2 %collective-permute-start.3 = (f32[256,256]{1,0:T(8,128)S(1)}, f32[256,256]{1,0:T(8,128)S(1)}, u32[]{:S(2)}, u32[]{:S(2)}) collective-permute-start(f32[256,256]{1,0:T(8,128)S(1)} %dynamic-slice_bitcast_fusion), channel_id=1, source_target_pairs={{0,4},{4,0},{8,12},{12,8},{16,20},{20,16},{24,28},{28,24},{1,5},{5... | collective-permute-start | bytes 786440 | tf_op jit(solution)/shard_map/ppermute | solution.py:361
  23.8 1.5 collective-permute-start
  74.7 4.8 %copy-start.1 = (bf16[4,256,256]{2,1,0:T(8,128)(2,1)S(1)}, bf16[4,256,256]{2,1,0:T(8,128)(2,1)}, u32[]{:S(2)}) copy-start(bf16[4,256,256]{2,1,0:T(8,128)(2,1)} %constant.110.rights) | copy-start | bytes 1572868
  74.7 4.8 %copy-start.2 = (bf16[2,512,256]{2,1,0:T(8,128)(2,1)S(1)}, bf16[2,512,256]{2,1,0:T(8,128)(2,1)}, u32[]{:S(2)}) copy-start(bf16[2,512,256]{2,1,0:T(8,128)(2,1)} %constant.115.lefts) | copy-start | bytes 1572868
  74.7 4.8 %copy-start.3 = (f32[2,128,256]{2,1,0:T(8,128)S(1)}, f32[2,128,256]{2,1,0:T(8,128)}, u32[]{:S(2)}) copy-start(f32[2,128,256]{2,1,0:T(8,128)} %constant.94.clone.subs) | copy-start | bytes 786436
  74.7 4.8 %copy-start.4 = (f32[2,1,128]{2,1,0:T(1,128)S(1)}, f32[2,1,128]{2,1,0:T(1,128)}, u32[]{:S(2)}) copy-start(f32[2,1,128]{2,1,0:T(1,128)} %constant.116.lanes) | copy-start | bytes 3076
  201.6 1.8 collective-permute-start.4
Sparse Core Ops, SparseCore 0:
  10.3 64.3 all-gather.3

commit v3 on v2

--- a/solution.py
+++ b/solution.py
@@ -67,12 +67,12 @@
     return both[:n] + (both[n:] + dot(t_both[:n], low))
 
 
-def gradient_kernel(col_ref, obj_ref, probe_ref, meas_ref, rights, lefts, lanes, subs, out_ref, far_ref, power_ref, acc_ref, patch_ref):
+def gradient_kernel(col_ref, obj_ref, kept_ref, came_ref, meas_ref, rights, lefts, lanes, subs, out_ref, far_ref, power_ref, acc_ref, patch_ref):
     n = meas_ref.shape[0]
     half = n // 2
     width = obj_ref.shape[2]
-    modes = probe_ref.shape[1]
-    col = col_ref[0]
+    modes = kept_ref.shape[0]
+    col, side = col_ref[0], col_ref[1]
     back = jnp.where(col == 0, 0, width - col)
     for part in range(2):
         patch_ref[part] = pltpu.roll(obj_ref[part], back, 1)[:, :n]
@@ -80,8 +80,12 @@
     acc_ref[...] = jnp.zeros_like(acc_ref)
     cat = jnp.concatenate
 
+    def probe_of(m):
+        kept, came = kept_ref[m], came_ref[m]
+        return jnp.where(side == 0, kept, came), jnp.where(side == 0, came, kept)
+
     def forward(m):
-        pr, pi = probe_ref[0, m], probe_ref[1, m]
+        pr, pi = probe_of(m)
         xr, xi = patch_ref[0], patch_ref[1]
         er = pr * xr - pi * xi
         ei = pr * xi + pi * xr
@@ -133,7 +137,7 @@
         tr, ti = br * wr + bi * wi, bi * wr - br * wi
         dr = cat([ar + tr, ar - tr], 1)
         di = cat([ai + ti, ai - ti], 1)
-        pr, pi = probe_ref[0, m], probe_ref[1, m]
+        pr, pi = probe_of(m)
         return pr * dr + pi * di, pr * di - pi * dr
 
     def backward_two(i, carry):
@@ -151,13 +155,13 @@
 
 def window_gradient(col, rows, probe, meas, consts):
     n = meas.shape[0]
-    modes = probe.shape[1]
+    modes = probe[0].shape[0]
     vmem = pl.BlockSpec(memory_space=pltpu.VMEM)
     flops = modes * 2 * 4 * 3 * 2 * n**3
     return pl.pallas_call(
         gradient_kernel,
         out_shape=jax.ShapeDtypeStruct(rows.shape, f32),
-        in_specs=[pl.BlockSpec(memory_space=pltpu.SMEM)] + [vmem] * 7,
+        in_specs=[pl.BlockSpec(memory_space=pltpu.SMEM)] + [vmem] * 8,
         out_specs=vmem,
         scratch_shapes=[
             pltpu.VMEM((modes, 2, n, n), f32),
@@ -168,7 +172,7 @@
         cost_estimate=pl.CostEstimate(flops=flops, bytes_accessed=8 * modes * n * n, transcendentals=n * n),
         compiler_params=pltpu.CompilerParams(vmem_limit_bytes=48 * 2**20),
         name="window_gradient",
-    )(col, rows, probe, meas, *consts)
+    )(col, rows, *probe, meas, *consts)
 
 
 def exchange_kernel(copies, slots, cells, g_ref, rows_ref, out_ref, pair, from_partner, from_prev, from_next, own, other, tile, tiles_a, sum_a, tiles_b, partner_sems, chain_sems, back_sems, a_send, a_recv, b_send, b_recv):
@@ -345,12 +349,8 @@
         lower = jnp.where(which == 0, 0, 3)
         return jnp.where(q % 2 == 0, upper, lower)
 
-    share = n // strips
-    piece = lax.dynamic_slice_in_dim(probe_modes, s * share, share, axis=2)
-    pieces = lax.all_gather(piece, ("strip", "mode"))
-    pieces = pieces.reshape(strips, group, 2, local, share, n)
-    probe = pieces.transpose(2, 1, 3, 0, 4, 5).reshape(2, group * local, n, n)
-
+    half_probe = lax.dynamic_index_in_dim(probe_modes, side, 0, keepdims=False)
+    kept = lax.all_gather(half_probe, "mode", tiled=True)
     below = lax.ppermute(object_field[:, :halo], "strip", [(i + 1, i) for i in range(strips - 1)])
     frame = jnp.concatenate([object_field, below], axis=1)
     own_rows = jnp.where(q % 2 == 0, frame[:, :stripe_rows], frame[:, halo:])
@@ -359,9 +359,15 @@
 
     pick = lambda which: lax.dynamic_index_in_dim(measured[0], window_of(which), 0, keepdims=False)
     meas = jnp.where(mine, pick(side), lax.ppermute(pick(1 - side), "strip", partner))
-    meas = meas.reshape(n // 2, 2, n // 2, 2).transpose(1, 0, 3, 2).reshape(n, n)
+    order = np.concatenate([np.arange(0, n, 2), np.arange(1, n, 2)])
+    place = jnp.asarray(np.eye(n)[order], f32)
+    exact = functools.partial(jnp.dot, precision=lax.Precision.HIGHEST)
+    meas = exact(exact(place, meas), place.T)
     at = lambda which: lax.dynamic_index_in_dim(positions[0, :, 1], window_of(which), 0)
     col = jnp.where(mine, at(side), lax.ppermute(at(1 - side), "strip", partner))
+    col = jnp.concatenate([col, side.reshape(1).astype(col.dtype)])
+    kept, meas, rows, col = lax.optimization_barrier((kept, meas, rows, col))
+    probe = (kept, lax.ppermute(kept, "strip", partner))
 
     cells = stripe_rows * strips * width
     for iteration in range(ITERS):

time: 212 us -> 194 us (0.915)
  local copies, waits for them, and re-layouts: 38.6 us -> 8 us
  waiting for transfers between devices: 24.5 us -> 35.9 us
  matrix products: 0 us -> 3.2 us
    reshape x2 -> x0, local copies, waits for them, and re-layouts: 22.9 us -> none  [the longest x1 18.1 us: body(): meas.reshape(n // 2, 2, n // 2, 2).transpose(1, 0, 3, 2).reshape(n, n)]
    transpose x1 -> x0, local copies, waits for them, and re-layouts: 9.5 us -> none  [body(): meas.reshape(n // 2, 2, n // 2, 2).transpose(1, 0, 3, 2).reshape(n, n)]
    all_gather x1, waiting for transfers between devices: 19.5 us -> 26.1 us  [body(): kept = lax.all_gather(half_probe, 'mode', tiled=True)]
    ppermute x0 -> x1, waiting for transfers between devices: none -> 4.5 us  [body(): probe = (kept, lax.ppermute(kept, 'strip', partner))]
    dot_general x0 -> x2, matrix products: none -> 3.2 us  [body(): meas = exact(exact(place, meas), place.T)]
    unnamed x11 -> x23, local copies, waits for them, and re-layouts: 1.26 us -> 3.67 us
  transfers between devices with their start and end apart: 6 -> 7, of which waited for: 4 -> 5; matrix products, arithmetic and copies ran while one was open for 16% -> 5% of each run, Pallas kernels for 0% -> 0%
where the time goes in v3:
time: 194 us
  Pallas kernels  101 us (52%)
  waiting for transfers between devices  35.9 us (19%)
  blocking collectives  19.7 us (10%)
  between operations  14.9 us (8%)
  starting transfers between devices  8.78 us (5%)
  local copies, waits for them, and re-layouts  8 us (4%)
  matrix products  3.2 us (2%)
  other arithmetic  2.48 us (1%)
    pallas_call x3, Pallas kernels, exchange(): pl.pallas_call(functools.partial(exchange_kernel, copies, slots, float(ce...  59.3 us
    pallas_call x3, Pallas kernels, window_gradient(): pl.pallas_call(gradient_kernel, out_shape=jax.ShapeDtypeStruct(rows.shape...  41.5 us
    all_gather x1, waiting for transfers between devices, body(): kept = lax.all_gather(half_probe, 'mode', tiled=True)  26.1 us
    all_gather x1, blocking collectives, body(): parts = lax.all_gather(mine_part, 'mode')[::copies]  19.7 us
    ppermute x1, starting transfers between devices, body(): theirs = lax.ppermute(own_rows, 'strip', partner)  6.9 us
    ppermute x1, waiting for transfers between devices, body(): probe = (kept, lax.ppermute(kept, 'strip', partner))  4.5 us
  transfers between devices with their start and end apart: 7, of which 5 were waited for; matrix products, arithmetic and copies ran while one was open for 5% of the time, Pallas kernels for 0%

profile of v3, /device:TPU:0, one launch (start us, length us, event | category | flops | bytes accessed | tf_op | source)
XLA Modules:
  0.0 193.8 jit_solution(11780141544268584503)
XLA Ops:
  6.5 0.0 copy-start
  6.5 0.0 copy-start.8
  6.5 0.0 all-gather.4.cloned.1.call-start
  6.5 1.2 copy-done
  7.8 0.8 dynamic-slice_bitcast_fusion
  8.6 0.0 copy-start.10
  8.6 0.0 copy-start.9
  8.6 0.0 all-gather.4.cloned.1.call-update
  8.6 1.1 slice.10
  9.7 1.3 collective-permute-start.1
  11.0 2.4 %collective-permute-done.1 = f32[2,128,384]{2,1,0:T(8,128)} collective-permute-done((f32[2,128,384]{2,1,0:T(8,128)S(1)}, f32[2,128,384]{2,1,0:T(8,128)}, u32[]{:S(2)}, u32[]{:S(2)}) %collective-permute-start.1) | collective-permute-done | bytes 393248 | tf_op jit(solution)/shard_map/ppermute | solution.py:354
  13.4 0.0 copy-done.8
  13.4 1.1 fusion
  14.5 0.0 copy-start.7
  14.5 6.9 %collective-permute-start.2 = (f32[2,256,384]{2,1,0:T(8,128)S(1)}, f32[2,256,384]{2,1,0:T(8,128)}, u32[]{:S(2)}, u32[]{:S(2)}) collective-permute-start(f32[2,256,384]{2,1,0:T(8,128)S(1)} %fusion), channel_id=1, source_target_pairs={{0,4},{4,0},{8,12},{12,8},{16,20},{20,16},{24,28},{28,24},{1,5},{5... | collective-permute-start | bytes 2359304 | tf_op jit(solution)/shard_map/ppermute | solution.py:357
  21.4 1.7 dynamic-slice_bitcast_fusion.1
  23.1 0.2 collective-permute-start
  23.3 0.0 copy-done.10
  23.3 0.6 constant_dynamic-slice_fusion.2
  23.9 0.3 collective-permute-start.3
  24.2 1.2 collective-permute-done.3
  26.7 0.1 pad_add_fusion.col_ref
  26.7 0.0 copy-start.3
  26.7 0.0 copy-start.4
  26.7 0.0 copy-start.5
  26.7 0.0 copy-start.6
  26.7 0.0 collective-permute-done
  26.8 0.0 copy-done.9
  26.8 1.7 fusion.1
  28.4 1.5 fusion.5.meas_ref
  30.0 0.0 copy-done.7
  30.0 0.0 collective-permute-done.2
  30.0 1.2 broadcast_select_fusion.obj_ref
  31.2 26.1 %all-gather.4.cloned.1.call-done = f32[1,8,256,256]{3,2,0,1:T(8,128)} async-done(((f32[1,2,256,256]{3,2,0,1:T(8,128)}), f32[1,8,256,256]{3,2,0,1:T(8,128)}) %all-gather.4.cloned.1.call-update) | async-done | bytes 2097168 | tf_op jit(solution)/shard_map/all_gather | solution.py:353
  57.3 0.0 collective-permute-start.4
  57.3 4.5 %collective-permute-done.4.came_ref = f32[8,256,256]{2,1,0:T(8,128)} collective-permute-done((f32[8,256,256]{2,1,0:T(8,128)}, f32[8,256,256]{2,1,0:T(8,128)}, u32[]{:S(2)}, u32[]{:S(2)}) %collective-permute-start.4) | collective-permute-done | bytes 2097184 | tf_op jit(solution)/shard_map/ppermute | solution.py:370
  61.8 0.0 copy-done.3
  61.8 0.0 copy-done.4
  61.8 0.0 copy-done.5
  61.8 0.0 copy-done.6
  61.8 0.0 copy-start.1
  61.9 1.6 copy-done.1
  63.4 13.8 %window_gradient.3 = f32[2,256,384]{2,1,0:T(8,128)S(1)} custom-call(s32[2]{0:T(128)S(1)} %pad_add_fusion.col_ref, f32[2,256,384]{2,1,0:T(8,128)S(1)} %broadcast_select_fusion.obj_ref, f32[8,256,256]{2,1,0:T(8,128)S(1)} %bitcast.34, f32[8,256,256]{2,1,0:T(8,128)} %collective-permute-done.4.came_ref, f32[256,256]{1,0:T(8,128)S(1)} %fusion.5.meas_ref, ...), custom_call_target="tpu_custom_call" | custom-call | flops 6442450944 | bytes 4194304 | tf_op jit(solution)/shard_map/window_gradient/pallas_call | solution.py:161
  77.3 0.0 copy-start.2
  77.3 19.8 %exchange.3.rows_ref = f32[2,2,2,64,384]{4,3,2,1,0:T(8,128)S(1)} custom-call(f32[2,2,2,64,384]{4,3,2,1,0:T(8,128)S(1)} %bitcast.31, f32[2,2,2,64,384]{4,3,2,1,0:T(8,128)S(1)} %bitcast.26), custom_call_target="tpu_custom_call" | custom-call | tf_op jit(solution)/shard_map/exchange/pallas_call | solution.py:312
  97.1 0.0 copy-done.2
  97.1 13.8 %window_gradient.4 = f32[2,256,384]{2,1,0:T(8,128)S(1)} custom-call(s32[2]{0:T(128)S(1)} %pad_add_fusion.col_ref, f32[2,256,384]{2,1,0:T(8,128)S(1)} %bitcast.28, f32[8,256,256]{2,1,0:T(8,128)S(1)} %bitcast.35, f32[8,256,256]{2,1,0:T(8,128)} %collective-permute-done.4.came_ref, f32[256,256]{1,0:T(8,128)S(1)} %fusion.5.meas_ref, ...), custom_call_target="tpu_custom_call" | custom-call | flops 6442450944 | bytes 4194304 | tf_op jit(solution)/shard_map/window_gradient/pallas_call | solution.py:161
  111.0 19.7 %exchange.4.rows_ref = f32[2,2,2,64,384]{4,3,2,1,0:T(8,128)S(1)} custom-call(f32[2,2,2,64,384]{4,3,2,1,0:T(8,128)S(1)} %bitcast.32, f32[2,2,2,64,384]{4,3,2,1,0:T(8,128)S(1)} %exchange.3.rows_ref), custom_call_target="tpu_custom_call" | custom-call | tf_op jit(solution)/shard_map/exchange/pallas_call | solution.py:312
  130.7 13.8 %window_gradient.5 = f32[2,256,384]{2,1,0:T(8,128)S(1)} custom-call(s32[2]{0:T(128)S(1)} %pad_add_fusion.col_ref, f32[2,256,384]{2,1,0:T(8,128)S(1)} %bitcast.27, f32[8,256,256]{2,1,0:T(8,128)S(1)} %bitcast.36, f32[8,256,256]{2,1,0:T(8,128)} %collective-permute-done.4.came_ref, f32[256,256]{1,0:T(8,128)S(1)} %fusion.5.meas_ref, ...), custom_call_target="tpu_custom_call" | custom-call | flops 6442450944 | bytes 4194304 | tf_op jit(solution)/shard_map/window_gradient/pallas_call | solution.py:161
  144.5 19.8 %exchange.5 = f32[2,2,2,64,384]{4,3,2,1,0:T(8,128)S(1)} custom-call(f32[2,2,2,64,384]{4,3,2,1,0:T(8,128)S(1)} %bitcast.30, f32[2,2,2,64,384]{4,3,2,1,0:T(8,128)S(1)} %exchange.4.rows_ref), custom_call_target="tpu_custom_call" | custom-call | tf_op jit(solution)/shard_map/exchange/pallas_call | solution.py:312
  164.3 19.7 %all-gather.1 = f32[8,64,384]{2,1,0:T(8,128)S(1)} all-gather(f32[2,64,384]{2,1,0:T(8,128)S(1)} %constant_dynamic-slice_fusion.1), channel_id=3, replica_groups=mesh['strip'=8,'mode'=4] {'mode'}, dimensions={0}, use_global_device_ids=true | all-gather | bytes 983040 | tf_op jit(solution)/shard_map/all_gather | solution.py:379
  184.1 0.1 collective-permute-start.5
  184.1 1.7 collective-permute-done.5
  185.8 0.1 dynamic-slice_select_fusion.1
  185.9 0.1 maximum_bitcast_fusion
  186.0 0.9 copy.15
  (3 shorter events, 0.1 us)
Async XLA Ops:
  6.5 1.2 copy-start
  6.5 6.9 %copy-start.8 = (f32[2,256,384]{2,1,0:T(8,128)S(1)}, f32[2,256,384]{2,1,0:T(8,128)}, u32[]{:S(2)}) copy-start(f32[2,256,384]{2,1,0:T(8,128)} %param.11) | copy-start | bytes 2359300
  6.5 50.8 %all-gather.4.cloned.1.call-start = ((), (), s32[]{:S(2)}) async-start(), calls=%async_computation | async-start | bytes 2621440 | tf_op jit(solution)/shard_map/all_gather | solution.py:353
  8.6 14.7 %copy-start.10 = (s32[1,4,2]{1,2,0:T(2,128)S(1)}, s32[1,4,2]{1,2,0:T(2,128)}, u32[]{:S(2)}) copy-start(s32[1,4,2]{1,2,0:T(2,128)} %param.14) | copy-start | bytes 100
  8.6 18.2 %copy-start.9 = (f32[256,256]{1,0:T(8,128)S(1)}, f32[256,256]{1,0:T(8,128)}, u32[]{:S(2)}) copy-start(f32[256,256]{1,0:T(8,128)} %constant.99.clone) | copy-start | bytes 786436
  9.7 3.7 %collective-permute-start.1 = (f32[2,128,384]{2,1,0:T(8,128)S(1)}, f32[2,128,384]{2,1,0:T(8,128)}, u32[]{:S(2)}, u32[]{:S(2)}) collective-permute-start(f32[2,128,384]{2,1,0:T(8,128)S(1)} %slice.10), channel_id=1, source_target_pairs={{4,0},{8,4},{12,8},{16,12},{20,16},{24,20},{28,24},{5,1},{9,5},{13... | collective-permute-start | bytes 1179656 | tf_op jit(solution)/shard_map/ppermute | solution.py:354
  14.5 15.5 %copy-start.7 = (f32[2,256,384]{2,1,0:T(8,128)}, f32[2,256,384]{2,1,0:T(8,128)S(1)}, u32[]{:S(2)}) copy-start(f32[2,256,384]{2,1,0:T(8,128)S(1)} %fusion) | copy-start | bytes 2359300
  14.5 15.5 %collective-permute-start.2 = (f32[2,256,384]{2,1,0:T(8,128)S(1)}, f32[2,256,384]{2,1,0:T(8,128)}, u32[]{:S(2)}, u32[]{:S(2)}) collective-permute-start(f32[2,256,384]{2,1,0:T(8,128)S(1)} %fusion), channel_id=1, source_target_pairs={{0,4},{4,0},{8,12},{12,8},{16,20},{20,16},{24,28},{28,24},{1,5},{5... | collective-permute-start | bytes 2359304 | tf_op jit(solution)/shard_map/ppermute | solution.py:357
  23.1 3.7 %collective-permute-start = (f32[256,256]{1,0:T(8,128)}, f32[256,256]{1,0:T(8,128)}, u32[]{:S(2)}, u32[]{:S(2)}) collective-permute-start(f32[256,256]{1,0:T(8,128)} %dynamic-slice_bitcast_fusion.1), channel_id=1, source_target_pairs={{0,4},{4,0},{8,12},{12,8},{16,20},{20,16},{24,28},{28,24},{1,5},{5... | collective-permute-start | bytes 786440 | tf_op jit(solution)/shard_map/ppermute | solution.py:361
  23.9 1.5 collective-permute-start.3
  26.7 35.1 %copy-start.3 = (bf16[4,256,256]{2,1,0:T(8,128)(2,1)S(1)}, bf16[4,256,256]{2,1,0:T(8,128)(2,1)}, u32[]{:S(2)}) copy-start(bf16[4,256,256]{2,1,0:T(8,128)(2,1)} %constant.115.rights) | copy-start | bytes 1572868
  26.7 35.1 %copy-start.4 = (bf16[2,512,256]{2,1,0:T(8,128)(2,1)S(1)}, bf16[2,512,256]{2,1,0:T(8,128)(2,1)}, u32[]{:S(2)}) copy-start(bf16[2,512,256]{2,1,0:T(8,128)(2,1)} %constant.120.lefts) | copy-start | bytes 1572868
  26.7 35.1 %copy-start.5 = (f32[2,128,256]{2,1,0:T(8,128)S(1)}, f32[2,128,256]{2,1,0:T(8,128)}, u32[]{:S(2)}) copy-start(f32[2,128,256]{2,1,0:T(8,128)} %constant.98.clone.subs) | copy-start | bytes 786436
  26.7 35.1 %copy-start.6 = (f32[2,1,128]{2,1,0:T(1,128)S(1)}, f32[2,1,128]{2,1,0:T(1,128)}, u32[]{:S(2)}) copy-start(f32[2,1,128]{2,1,0:T(1,128)} %constant.121.lanes) | copy-start | bytes 3076
  57.3 4.5 %collective-permute-start.4 = (f32[8,256,256]{2,1,0:T(8,128)}, f32[8,256,256]{2,1,0:T(8,128)}, u32[]{:S(2)}, u32[]{:S(2)}) collective-permute-start(f32[8,256,256]{2,1,0:T(8,128)} %bitcast.33), channel_id=1, source_target_pairs={{0,4},{4,0},{8,12},{12,8},{16,20},{20,16},{24,28},{28,24},{1,5},{5... | collective-permute-start | bytes 6291464 | tf_op jit(solution)/shard_map/ppermute | solution.py:370
  61.8 1.6 copy-start.1
  77.3 19.8 %copy-start.2 = (f32[1,8,256,256]{3,2,0,1:T(8,128)S(1)}, f32[1,8,256,256]{3,2,0,1:T(8,128)}, u32[]{:S(2)}) copy-start(f32[1,8,256,256]{3,2,0,1:T(8,128)} %all-gather.4.cloned.1.call-done) | copy-start | bytes 6291460
  184.1 1.8 collective-permute-start.5
Sparse Core Ops, SparseCore 0:
  8.9 48.3 all-gather.3
